TPU v7x, 32 devices: a whole 2x2x4 slice. The times are simulated.
32 devices in a mesh: fsdp: 4 (over y, x), ctx: 4 (over z), tp: 2 (over core).
Axes of the slice: x: 2, y: 2, z: 4, core: 2. Of those that a mesh axis runs over, the one named last changes fastest.
Arguments:
- tokens: bfloat16 [8, 1024, 2048], P('fsdp', 'ctx'), may hold values from -6 to 6
- cotangent: bfloat16 [8, 1024, 2048], P('fsdp', 'ctx'), may hold values from -6 to 6
- prefix_len: int32 [8], P('fsdp'), may hold values from 102 to 512
- group_order: int32 [8], replicated, may hold values from 0 to 7, each once
- ln_gain: bfloat16 [2048], replicated, may hold values from 0.25 to 1.75
- ln_bias: bfloat16 [2048], replicated, may hold values from -4 to 4
- query_weight: bfloat16 [2048, 2048], P('fsdp', 'tp'), may hold values from -0.125 to 0.125
- query_bias: bfloat16 [2048], P('tp'), may hold values from -4 to 4
- key_weight: bfloat16 [2048, 2048], P('fsdp', 'tp'), may hold values from -0.125 to 0.125
- key_bias: bfloat16 [2048], P('tp'), may hold values from -4 to 4
- value_weight: bfloat16 [2048, 2048], P('fsdp', 'tp'), may hold values from -0.125 to 0.125
- value_bias: bfloat16 [2048], P('tp'), may hold values from -4 to 4
- out_weight: bfloat16 [2048, 2048], P('fsdp', 'tp'), may hold values from -1 to 1
- out_bias: bfloat16 [2048], replicated, may hold values from -4 to 4
- up_weight: bfloat16 [2048, 8192], P('fsdp', 'tp'), may hold values from -0.125 to 0.125
- up_bias: bfloat16 [8192], P('tp'), may hold values from -4 to 4
- down_weight: bfloat16 [2048, 8192], P('fsdp', 'tp'), may hold values from -0.0625 to 0.0625
- down_bias: bfloat16 [2048], replicated, may hold values from -4 to 4
Outputs:
- output: bfloat16 [8, 1024, 2048], P('fsdp', 'ctx')
- input_grad: bfloat16 [8, 1024, 2048], P('fsdp', 'ctx')
- ln_gain_grad: float32 [2048], replicated
- ln_bias_grad: float32 [2048], replicated
- query_weight_grad: float32 [2048, 2048], P('fsdp', 'tp')
- query_bias_grad: float32 [2048], P('tp')
- key_weight_grad: float32 [2048, 2048], P('fsdp', 'tp')
- key_bias_grad: float32 [2048], P('tp')
- value_weight_grad: float32 [2048, 2048], P('fsdp', 'tp')
- value_bias_grad: float32 [2048], P('tp')
- out_weight_grad: float32 [2048, 2048], P('fsdp', 'tp')
- up_weight_grad: float32 [2048, 8192], P('fsdp', 'tp')
- up_bias_grad: float32 [8192], P('tp')
- down_weight_grad: float32 [2048, 8192], P('fsdp', 'tp')
- out_biases_grad: float32 [2048], replicated
Inputs may be any that keep to these rules, and one draw needn't show every extreme that they name: Each number of 0 to 7 appears once; storage rows k * 128 to k * 128 + 127 of every sequence hold positions group_order[k] * 128 onwards.
All inputs are finite; a program needn't handle non-finite values.
Results may differ from a plain program's by a relative error of at most 0.012.
Values may be sent and summed in bfloat16 or wider, within the bound.
No kernel may reach another device: no remote copies, remote signals or barrier semaphores. Data moves between devices by JAX's collectives and lax.ppermute only.
A program may use at most 448 MiB of HBM per device.

v0:
```python
import jax
import jax.numpy as jnp
from jax import lax
from jax.sharding import PartitionSpec as P

HD = 64
ROT = 32
SEQ_LEN = 1024
masked_fill = -1e30
norm_eps = 1e-05


def positions(group_order, row_start, row_count, group_len):
    row_index = row_start + jnp.arange(row_count, dtype=jnp.int32)
    slot_index = row_index // group_len
    offset = row_index - slot_index * group_len
    matches = slot_index[:, None] == jnp.arange(group_order.shape[0], dtype=jnp.int32)[None, :]
    anchor = jnp.sum(jnp.where(matches, group_order[None, :], 0), axis=1)
    return anchor * group_len + offset


def rotary_tables(places):
    half_rot = ROT // 2
    frequency = jnp.power(10000.0, -2.0 * jnp.arange(half_rot, dtype=jnp.float32) / ROT)
    angles = places.astype(jnp.float32)[:, None] * frequency[None, :]
    return (jnp.cos(angles), jnp.sin(angles))


def rotate(tensor, cosine, sine_vals):
    half_rot = cosine.shape[-1]
    front_part = tensor[..., :half_rot]
    back_part = tensor[..., half_rot : 2 * half_rot]
    rest_part = tensor[..., 2 * half_rot :]
    cosine_rows = cosine[:, None, :]
    sine_rows = sine_vals[:, None, :]
    return jnp.concatenate(
        [
            front_part * cosine_rows - back_part * sine_rows,
            back_part * cosine_rows + front_part * sine_rows,
            rest_part,
        ],
        axis=-1,
    )


def gelu_tanh(values_in):
    return jax.nn.gelu(values_in, approximate=True)


def local(
    tokens,
    cotangent,
    prefix_len,
    group_order,
    ln_gain,
    ln_bias,
    query_weight,
    query_bias,
    key_weight,
    key_bias,
    value_weight,
    value_bias,
    out_weight,
    out_bias,
    up_weight,
    up_bias,
    down_weight,
    down_bias,
):
    seq_count, local_rows, model_width = tokens.shape
    token_count = seq_count * local_rows
    inner_width = query_weight.shape[1]
    local_heads = inner_width // HD
    hidden_units = up_weight.shape[1]
    group_len = SEQ_LEN // group_order.shape[0]
    score_scale = HD ** (-0.5)
    own_place = positions(group_order, lax.axis_index("ctx") * local_rows, local_rows, group_len)
    key_place = positions(group_order, 0, SEQ_LEN, group_len)
    cosine, sine_vals = rotary_tables(own_place)
    allowed = (key_place[None, None, None, :] <= own_place[None, None, :, None]) | (
        key_place[None, None, None, :] < prefix_len[:, None, None, None]
    )
    gathered = (
        lax.all_gather(query_weight, "fsdp", axis=0, tiled=True),
        lax.all_gather(key_weight, "fsdp", axis=0, tiled=True),
        lax.all_gather(value_weight, "fsdp", axis=0, tiled=True),
        lax.all_gather(out_weight, "fsdp", axis=0, tiled=True),
        lax.all_gather(up_weight, "fsdp", axis=0, tiled=True),
        lax.all_gather(down_weight, "fsdp", axis=0, tiled=True),
    )
    w_query, w_key, w_value, w_out, w_up, w_down = gathered
    inputs = tokens.reshape(token_count, model_width).astype(jnp.float32)
    centre = jnp.mean(inputs, axis=-1, keepdims=True)
    centred = inputs - centre
    inv_std = lax.rsqrt(jnp.mean(centred * centred, axis=-1, keepdims=True) + norm_eps)
    normed = centred * inv_std
    norm_gain = ln_gain.astype(jnp.float32)
    hidden = (normed * norm_gain + ln_bias.astype(jnp.float32)).astype(jnp.bfloat16)

    def project(weight, bias_vec):
        return jnp.dot(hidden, weight, preferred_element_type=jnp.float32) + bias_vec.astype(
            jnp.float32
        )

    query_rot = rotate(
        project(w_query, query_bias).reshape(seq_count, local_rows, local_heads, HD),
        cosine,
        sine_vals,
    ).astype(jnp.bfloat16)
    key_rot = (
        rotate(
            project(w_key, key_bias).reshape(seq_count, local_rows, local_heads, HD),
            cosine,
            sine_vals,
        )
        .astype(jnp.bfloat16)
        .reshape(seq_count, local_rows, inner_width)
    )
    value_rows = (
        project(w_value, value_bias)
        .astype(jnp.bfloat16)
        .reshape(seq_count, local_rows, inner_width)
    )
    keys_all, values_all = (
        lax.all_gather(key_rot, "ctx", axis=1, tiled=True),
        lax.all_gather(value_rows, "ctx", axis=1, tiled=True),
    )

    def scores_for(key_block):
        key_heads = key_block.reshape(seq_count, key_block.shape[1], local_heads, HD)
        raw_scores = (
            jnp.einsum("bqhd,bkhd->bhqk", query_rot, key_heads, preferred_element_type=jnp.float32)
            * score_scale
        )
        return jnp.where(allowed, raw_scores, masked_fill)

    masked = scores_for(keys_all)
    row_max = jnp.max(masked, axis=-1, keepdims=True)
    exponent = jnp.exp(masked - row_max)
    row_total = jnp.sum(exponent, axis=-1, keepdims=True)
    attn_probs = (exponent / row_total).astype(jnp.bfloat16)
    log_total = row_max + jnp.log(row_total)
    value_heads = values_all.reshape(seq_count, values_all.shape[1], local_heads, HD)
    context = jnp.einsum(
        "bhqk,bkhd->bqhd", attn_probs, value_heads, preferred_element_type=jnp.float32
    )
    context = context.reshape(token_count, inner_width).astype(jnp.bfloat16)
    up_proj = project(w_up, up_bias)
    activated = gelu_tanh(up_proj).astype(jnp.bfloat16)
    partial_out = jnp.dot(context, w_out.T, preferred_element_type=jnp.float32) + jnp.dot(
        activated, w_down.T, preferred_element_type=jnp.float32
    )
    branches = lax.psum(partial_out, "tp")
    output = inputs + branches + out_bias.astype(jnp.float32) + down_bias.astype(jnp.float32)
    output = output.astype(jnp.bfloat16).reshape(seq_count, local_rows, model_width)
    back_query, back_key, back_value, back_out, back_up, back_down = (
        lax.all_gather(query_weight, "fsdp", axis=0, tiled=True),
        lax.all_gather(key_weight, "fsdp", axis=0, tiled=True),
        lax.all_gather(value_weight, "fsdp", axis=0, tiled=True),
        lax.all_gather(out_weight, "fsdp", axis=0, tiled=True),
        lax.all_gather(up_weight, "fsdp", axis=0, tiled=True),
        lax.all_gather(down_weight, "fsdp", axis=0, tiled=True),
    )
    keys_back, values_back = (
        lax.all_gather(key_rot, "ctx", axis=1, tiled=True),
        lax.all_gather(value_rows, "ctx", axis=1, tiled=True),
    )
    grad_out = cotangent.reshape(token_count, model_width)
    grad_context = jnp.dot(grad_out, back_out, preferred_element_type=jnp.float32).astype(
        jnp.bfloat16
    )
    grad_heads = grad_context.reshape(seq_count, local_rows, local_heads, HD)
    key_heads_back = keys_back.reshape(seq_count, keys_back.shape[1], local_heads, HD)
    value_heads_back = values_back.reshape(seq_count, values_back.shape[1], local_heads, HD)
    probs_back = jnp.exp(scores_for(keys_back) - log_total)
    grad_probs = jnp.einsum(
        "bqhd,bkhd->bhqk", grad_heads, value_heads_back, preferred_element_type=jnp.float32
    )
    row_delta = jnp.sum(probs_back * grad_probs, axis=-1, keepdims=True)
    grad_scores = (probs_back * (grad_probs - row_delta)).astype(jnp.bfloat16)
    probs_low = probs_back.astype(jnp.bfloat16)
    grad_query_rot = (
        jnp.einsum(
            "bhqk,bkhd->bqhd", grad_scores, key_heads_back, preferred_element_type=jnp.float32
        )
        * score_scale
    )
    row_count = local_rows * lax.axis_size("ctx")
    grad_key_part = (
        jnp.einsum("bhqk,bqhd->kbhd", grad_scores, query_rot, preferred_element_type=jnp.float32)
        * score_scale
    )
    grad_value_part = jnp.einsum(
        "bhqk,bqhd->kbhd", probs_low, grad_heads, preferred_element_type=jnp.float32
    )
    key_grads = lax.psum_scatter(
        jnp.concatenate(
            [
                grad_key_part.reshape(row_count, seq_count, inner_width),
                grad_value_part.reshape(row_count, seq_count, inner_width),
            ],
            axis=2,
        ),
        "ctx",
        scatter_dimension=0,
        tiled=True,
    )
    key_grads = jnp.transpose(key_grads, (1, 0, 2))
    key_grad_rot = key_grads[:, :, :inner_width].reshape(seq_count, local_rows, local_heads, HD)
    grad_value = (
        key_grads[:, :, inner_width:].astype(jnp.bfloat16).reshape(token_count, inner_width)
    )
    grad_query = (
        rotate(grad_query_rot, cosine, -sine_vals)
        .astype(jnp.bfloat16)
        .reshape(token_count, inner_width)
    )
    grad_key = (
        rotate(key_grad_rot, cosine, -sine_vals)
        .astype(jnp.bfloat16)
        .reshape(token_count, inner_width)
    )
    grad_activated = jnp.dot(grad_out, back_down, preferred_element_type=jnp.float32)
    gelu_pull = jax.vjp(gelu_tanh, up_proj)[1]
    grad_up = gelu_pull(grad_activated)[0].astype(jnp.bfloat16)
    partial_hidden = (
        jnp.dot(grad_query, back_query.T, preferred_element_type=jnp.float32)
        + jnp.dot(grad_key, back_key.T, preferred_element_type=jnp.float32)
        + jnp.dot(grad_value, back_value.T, preferred_element_type=jnp.float32)
        + jnp.dot(grad_up, back_up.T, preferred_element_type=jnp.float32)
    )
    grad_hidden = lax.psum(partial_hidden, "tp")
    grad_scaled = grad_hidden * norm_gain
    grad_normed = inv_std * (
        grad_scaled
        - jnp.mean(grad_scaled, axis=-1, keepdims=True)
        - normed * jnp.mean(grad_scaled * normed, axis=-1, keepdims=True)
    )
    grad_float = grad_out.astype(jnp.float32)
    input_grad = (
        (grad_float + grad_normed).astype(jnp.bfloat16).reshape(seq_count, local_rows, model_width)
    )
    small_terms = (
        jnp.sum(grad_hidden * normed, axis=0),
        jnp.sum(grad_hidden, axis=0),
        jnp.sum(grad_query, axis=0, dtype=jnp.float32),
        jnp.sum(grad_key, axis=0, dtype=jnp.float32),
        jnp.sum(grad_value, axis=0, dtype=jnp.float32),
        jnp.sum(grad_up, axis=0, dtype=jnp.float32),
        jnp.sum(grad_float, axis=0),
    )
    gain_grad, shift_grad, qbias_grad, kbias_grad, vbias_grad, ubias_grad, obias_grad = lax.psum(
        (
            small_terms[0],
            small_terms[1],
            small_terms[2],
            small_terms[3],
            small_terms[4],
            small_terms[5],
            small_terms[6],
        ),
        ("fsdp", "ctx"),
    )
    grads_in = jnp.concatenate([grad_query, grad_key, grad_value, grad_up], axis=1)
    acts_out = jnp.concatenate([context, activated], axis=1)
    left_part = jnp.einsum("tc,tn->cn", hidden, grads_in, preferred_element_type=jnp.float32)
    right_part = jnp.einsum("tc,tn->cn", grad_out, acts_out, preferred_element_type=jnp.float32)
    scattered = lax.psum_scatter(
        jnp.concatenate([left_part, right_part], axis=1), "fsdp", scatter_dimension=0, tiled=True
    )
    weight_grads = lax.psum(scattered, "ctx")
    edge_two = 2 * inner_width
    edge_three = 3 * inner_width
    edge_four = edge_three + hidden_units
    edge_five = edge_four + inner_width
    return (
        output,
        input_grad,
        gain_grad,
        shift_grad,
        weight_grads[:, :inner_width],
        qbias_grad,
        weight_grads[:, inner_width:edge_two],
        kbias_grad,
        weight_grads[:, edge_two:edge_three],
        vbias_grad,
        weight_grads[:, edge_four:edge_five],
        weight_grads[:, edge_three:edge_four],
        ubias_grad,
        weight_grads[:, edge_five:],
        obias_grad,
    )


def solution(mesh):
    return jax.shard_map(
        local,
        mesh=mesh,
        in_specs=(
            P("fsdp", "ctx", None),
            P("fsdp", "ctx", None),
            P("fsdp"),
            P(),
            P(),
            P(),
            P("fsdp", "tp"),
            P("tp"),
            P("fsdp", "tp"),
            P("tp"),
            P("fsdp", "tp"),
            P("tp"),
            P("fsdp", "tp"),
            P(),
            P("fsdp", "tp"),
            P("tp"),
            P("fsdp", "tp"),
            P(),
        ),
        out_specs=(
            P("fsdp", "ctx", None),
            P("fsdp", "ctx", None),
            P(),
            P(),
            P("fsdp", "tp"),
            P("tp"),
            P("fsdp", "tp"),
            P("tp"),
            P("fsdp", "tp"),
            P("tp"),
            P("fsdp", "tp"),
            P("fsdp", "tp"),
            P("tp"),
            P("fsdp", "tp"),
            P(),
        ),
        check_vma=False,
    )
```

profile of v0, /device:TPU:0, one launch (start us, length us, event | category | flops | bytes accessed | tf_op | source)
XLA Modules:
  0.0 2836.2 jit_solution(8669938643243681293)
XLA Ops:
  14.0 51.3 %all-gather.9.cloned.1.call-done = bf16[2048,1024]{1,0:T(8,128)(2,1)} async-done(((bf16[512,1024]{1,0:T(8,128)(2,1)}), bf16[2048,1024]{1,0:T(8,128)(2,1)}) %all-gather.9.cloned.1.call-update) | async-done | bytes 4194320 | tf_op jit(solution)/shard_map/all_gather | solution.py:86
  65.3 6.1 add_convert_fusion
  72.7 47.3 %all-gather.15.cloned.1.call-done = bf16[2048,1024]{1,0:T(8,128)(2,1)} async-done(((bf16[512,1024]{1,0:T(8,128)(2,1)}), bf16[2048,1024]{1,0:T(8,128)(2,1)}) %all-gather.15.cloned.1.call-update) | async-done | bytes 4194320 | tf_op jit(solution)/shard_map/all_gather | solution.py:85
  119.9 5.8 convolution_add_fusion.1
  125.8 2.9 copy.73
  128.6 3.7 reshape.388
  134.8 39.8 %all-gather.13.cloned.1.call-done = bf16[2048,1024]{1,0:T(8,128)(2,1)} async-done(((bf16[512,1024]{1,0:T(8,128)(2,1)}), bf16[2048,1024]{1,0:T(8,128)(2,1)}) %all-gather.13.cloned.1.call-update) | async-done | bytes 4194320 | tf_op jit(solution)/shard_map/all_gather | solution.py:84
  174.5 5.8 convolution_add_fusion.2
  180.3 4.5 reshape.399
  184.9 8.3 fusion.57
  193.2 3.6 copy.98
  196.8 3.5 copy.97
  210.7 18.2 all-gather.19.cloned.1.call-done
  228.9 5.2 convolution_convert_fusion
  242.1 69.7 %all-gather.11.cloned.1.call-done = bf16[2,1024,1024]{2,1,0:T(8,128)(2,1)} async-done(((bf16[2,256,1024]{2,1,0:T(8,128)(2,1)}), bf16[2,1024,1024]{2,1,0:T(8,128)(2,1)}) %all-gather.11.cloned.1.call-update) | async-done | bytes 4194320 | tf_op jit(solution)/shard_map/all_gather | solution.py:126
  311.7 6.2 copy.68
  318.0 74.9 %all-gather.17.cloned.1.call-done = bf16[2,1024,1024]{1,2,0:T(8,128)(2,1)} async-done(((bf16[2,256,1024]{1,2,0:T(8,128)(2,1)}), bf16[2,1024,1024]{1,2,0:T(8,128)(2,1)}) %all-gather.17.cloned.1.call-update) | async-done | bytes 4194320 | tf_op jit(solution)/shard_map/all_gather | solution.py:125
  392.9 20.1 fusion.59
  412.9 14.6 fusion
  427.5 22.3 multiply_reduce_fusion
  449.8 29.6 %multiply_convert_fusion = bf16[2,16,256,1024]{3,2,1,0:T(8,128)(2,1)} fusion(f32[2,16,256,1024]{3,2,1,0:T(8,128)} %get-tuple-element.72, f32[2,16,256,1024]{3,2,1,0:T(8,128)} %get-tuple-element.70, f32[2,16,256]{2,1,0:T(8,128)S(1)} %get-tuple-element.71, f32[2,16,256]{2,1,0:T(8,128)S(1)} %log_add_fusion), kind=kLoop, calls=%fused_computation.1 | loop fusion | flops 33554432 | bytes 83951616 | tf_op jit(solution)/shard_map/convert_element_type | solution.py:180
  479.4 12.2 broadcast_multiply_fusion
  491.6 17.0 fusion.2
  508.6 11.9 pad_maximum_fusion.1
  521.2 15.1 fusion.43
  539.9 13.7 multiply_bitcast_fusion
  554.9 14.4 fusion.61
  569.3 140.3 %all-gather.23.cloned.1.call-done = bf16[2048,4096]{1,0:T(8,128)(2,1)} async-done(((bf16[512,4096]{1,0:T(8,128)(2,1)}), bf16[2048,4096]{1,0:T(8,128)(2,1)}) %all-gather.23.cloned.1.call-update) | async-done | bytes 16777232 | tf_op jit(solution)/shard_map/all_gather | solution.py:89
  709.6 22.4 convert_reduce_fusion
  732.1 22.1 convolution_bitcast_fusion
  754.2 238.2 %reduce-scatter.3.cloned.1.call-done = f32[256,2,2048]{0,2,1:T(8,128)} async-done(((f32[1024,2,2048]{0,2,1:T(8,128)}), f32[256,2,2048]{0,2,1:T(8,128)}) %reduce-scatter.3.cloned.1.call-update) | async-done | bytes 4194320 | tf_op jit(solution)/shard_map/reduce_scatter | solution.py:196
  992.3 4.0 convert_reduce_fusion.3
  1008.6 26.3 fusion.13
  1034.9 65.5 %pad_maximum_fusion = f32[2048,12288]{1,0:T(8,128)} fusion(f32[2048,5120]{1,0:T(8,128)} %convolution_bitcast_fusion, f32[2048,7168]{1,0:T(8,128)} %fusion.13), kind=kLoop, calls=%fused_computation | loop fusion | flops 25165824 | bytes 201326592 | tf_op jit(solution)/shard_map/concatenate | solution.py:269
  1101.7 6.7 fusion.60
  1108.4 16.2 convolution_add_fusion
  1124.6 4.4 fusion.63
  1129.0 4.4 fusion.62
  1133.4 4.4 fusion.64
  1137.8 18.3 add_add_fusion
  1156.2 773.7 %reduce-scatter.5.cloned.1.call-done = f32[512,12288]{1,0:T(8,128)} async-done(((f32[2048,12288]{1,0:T(8,128)}), f32[512,12288]{1,0:T(8,128)}) %reduce-scatter.5.cloned.1.call-update) | async-done | bytes 25165840 | tf_op jit(solution)/shard_map/reduce_scatter | solution.py:268
  1932.8 39.2 %all-reduce.7.cloned.1.call-done = (f32[512,2048]{1,0:T(8,128)}, f32[512,2048]{1,0:T(8,128)}) async-done(((f32[512,2048]{1,0:T(8,128)}, f32[512,2048]{1,0:T(8,128)}), (f32[512,2048]{1,0:T(8,128)}, f32[512,2048]{1,0:T(8,128)})) %all-reduce.7.cloned.1.call-update) | async-done | bytes 8388624 | tf_op jit(solution)/shard_map/psum | solution.py:153
  1972.0 3.6 fusion.38
  1975.7 82.3 %all-reduce = (f32[2048]{0:T(1024)}, f32[2048]{0:T(1024)}, f32[1024]{0:T(1024)}, f32[1024]{0:T(1024)}, f32[1024]{0:T(1024)}, /*index=5*/f32[4096]{0:T(1024)}, f32[2048]{0:T(1024)}) all-reduce(f32[2048]{0:T(1024)S(1)} %get-tuple-element.15, f32[2048]{0:T(1024)S(1)} %get-tuple-element.18, ...), channel_id=1, replica_groups=mesh['fsdp'=4,'ctx'=4,'tp'=2] {'fsdp','ctx'}, use_global_device_ids=true, to_apply=%region_13.14 | all-reduce | flops 13312 | bytes 106496 | tf_op jit(solution)/shard_map/psum | solution.py:252
  2058.0 6.8 fusion.37
  2064.8 745.8 %all-reduce.5.cloned.1.call-done = f32[512,12288]{1,0:T(8,128)} async-done(((f32[512,12288]{1,0:T(8,128)}), f32[512,12288]{1,0:T(8,128)}) %all-reduce.5.cloned.1.call-update) | async-done | bytes 25165840 | tf_op jit(solution)/shard_map/psum | solution.py:271
  2810.6 7.5 fusion.56
  2818.1 11.1 fusion.55
  (166 shorter events, 50.4 us)
Async XLA Ops:
  7.2 2.9 copy-start
  7.2 4.0 copy-start.34
  7.2 4.0 copy-start.30
  7.2 4.0 copy-start.31
  7.2 58.1 %all-gather.9.cloned.1.call-start = ((), (), s32[]{:S(2)}) async-start(), calls=%async_computation.2 | async-start | bytes 5242880 | tf_op jit(solution)/shard_map/all_gather | solution.py:86
  8.0 112.0 %all-gather.15.cloned.1.call-start = ((), (), s32[]{:S(2)}) async-start(), calls=%async_computation.5 | async-start | bytes 5242880 | tf_op jit(solution)/shard_map/all_gather | solution.py:85
  8.7 165.8 %all-gather.13.cloned.1.call-start = ((), (), s32[]{:S(2)}) async-start(), calls=%async_computation.4 | async-start | bytes 5242880 | tf_op jit(solution)/shard_map/all_gather | solution.py:84
  9.4 219.5 %all-gather.19.cloned.1.call-start = ((), (), s32[]{:S(2)}) async-start(), calls=%async_computation.7 | async-start | bytes 5242880 | tf_op jit(solution)/shard_map/all_gather | solution.py:87
  10.0 301.7 %all-gather.11.cloned.1.call-start = ((), (), s32[]{:S(2)}) async-start(), calls=%async_computation.3 | async-start | bytes 5242880 | tf_op jit(solution)/shard_map/all_gather | solution.py:126
  14.0 57.7 %copy-start.35 = (bf16[1024]{0:T(1024)(128)(2,1)S(1)}, bf16[1024]{0:T(1024)(128)(2,1)}, u32[]{:S(2)}) copy-start(bf16[1024]{0:T(1024)(128)(2,1)} %param.25) | copy-start | bytes 6148
  14.0 57.8 %copy-start.36 = (bf16[1024]{0:T(1024)(128)(2,1)S(1)}, bf16[1024]{0:T(1024)(128)(2,1)}, u32[]{:S(2)}) copy-start(bf16[1024]{0:T(1024)(128)(2,1)} %param.27) | copy-start | bytes 6148
  14.0 57.8 %copy-start.37 = (s32[8]{0:T(128)S(1)}, s32[8]{0:T(128)}, u32[]{:S(2)}) copy-start(s32[8]{0:T(128)} %param.21) | copy-start | bytes 100
  14.0 105.9 %copy-start.3 = (bf16[512,2048]{1,0:T(8,128)(2,1)S(1)}, bf16[512,2048]{1,0:T(8,128)(2,1)}, u32[]{:S(2)}) copy-start(bf16[512,2048]{1,0:T(8,128)(2,1)} %fusion.32) | copy-start | bytes 6291460
  71.5 321.4 %all-gather.17.cloned.1.call-start = ((), (), s32[]{:S(2)}) async-start(), calls=%async_computation.6 | async-start | bytes 5242880 | tf_op jit(solution)/shard_map/all_gather | solution.py:125
  72.7 128.0 %copy-start.16 = (f32[256,16]{0,1:T(8,128)}, f32[256,16]{0,1:T(8,128)S(1)}, u32[]{:S(2)}) copy-start(f32[256,16]{0,1:T(8,128)S(1)} %get-tuple-element.68) | copy-start | bytes 49156
  193.2 7.1 copy-start.5
  200.3 2.0 copy-start.15
  204.9 1.7 copy-start.38
  204.9 350.0 %all-gather.21.cloned.1.call-start = ((), (), s32[]{:S(2)}) async-start(), calls=%async_computation.8 | async-start | bytes 20971520 | tf_op jit(solution)/shard_map/all_gather | solution.py:88
  205.7 503.9 %all-gather.23.cloned.1.call-start = ((), (), s32[]{:S(2)}) async-start(), calls=%async_computation.9 | async-start | bytes 20971520 | tf_op jit(solution)/shard_map/all_gather | solution.py:89
  206.4 785.9 %reduce-scatter.3.cloned.1.call-start = ((), (), s32[]{:S(2)}) async-start(), calls=%async_computation.10 | async-start | bytes 20971520 | tf_op jit(solution)/shard_map/reduce_scatter | solution.py:196
  242.1 150.8 %copy-start.7 = (bf16[2,256,16,32]{1,3,2,0:T(8,128)(2,1)S(1)}, bf16[2,256,16,32]{1,3,2,0:T(8,128)(2,1)}, u32[]{:S(2)}) copy-start(bf16[2,256,16,32]{1,3,2,0:T(8,128)(2,1)} %copy.99) | copy-start | bytes 1572868
  242.1 150.8 %copy-start.8 = (pred[2,256,1024]{2,1,0:T(8,128)(4,1)S(1)}, pred[2,256,1024]{2,1,0:T(8,128)(4,1)}, u32[]{:S(2)}) copy-start(pred[2,256,1024]{2,1,0:T(8,128)(4,1)} %broadcast_or_fusion) | copy-start | bytes 1572868
  242.1 150.8 %copy-start.14 = (bf16[2,256,16,16]{1,3,2,0:T(8,128)(2,1)S(1)}, bf16[2,256,16,16]{1,3,2,0:T(8,128)(2,1)}, u32[]{:S(2)}) copy-start(bf16[2,256,16,16]{1,3,2,0:T(8,128)(2,1)} %get-tuple-element.57) | copy-start | bytes 786436
  412.9 14.6 copy-start.2
  520.5 1409.4 %reduce-scatter.5.cloned.1.call-start = ((), (), s32[]{:S(2)}) async-start(), calls=%async_computation.11 | async-start | bytes 125829120 | tf_op jit(solution)/shard_map/reduce_scatter | solution.py:268
  537.6 1.0 copy-start.9
  539.9 15.0 copy-start.4
  754.1 242.3 %copy-start.17 = (f32[256,16]{0,1:T(8,128)S(1)}, f32[256,16]{0,1:T(8,128)}, u32[]{:S(2)}) copy-start(f32[256,16]{0,1:T(8,128)} %copy-done.16) | copy-start | bytes 49156
  754.1 242.3 %copy-start.20 = (f32[256,16]{0,1:T(8,128)S(1)}, f32[256,16]{0,1:T(8,128)}, u32[]{:S(2)}) copy-start(f32[256,16]{0,1:T(8,128)} %get-tuple-element.66) | copy-start | bytes 49156
  992.3 4.1 copy-start.6
  1000.0 7.1 copy-start.11
  1100.5 1.2 copy-start.10
  1100.5 871.5 %all-reduce.7.cloned.1.call-start = ((), (), s32[]{:S(2)}) async-start(), calls=%async_computation.13 | async-start | bytes 16777216 | tf_op jit(solution)/shard_map/psum | solution.py:153
  1108.4 16.2 copy-start.12
  1108.4 16.2 copy-start.40
  1124.6 4.4 copy-start.13
  1124.6 4.4 copy-start.41
  1129.0 4.4 copy-start.39
  1156.2 1654.4 %all-reduce.5.cloned.1.call-start = ((), (), s32[]{:S(2)}) async-start(), calls=%async_computation.12 | async-start | bytes 50331648 | tf_op jit(solution)/shard_map/psum | solution.py:271
  1929.9 2.7 copy-start.26
  1929.9 2.8 copy-start.25
  1929.9 42.1 %copy-start.1 = (bf16[2,256,2048]{2,1,0:T(8,128)(2,1)S(1)}, bf16[2,256,2048]{2,1,0:T(8,128)(2,1)}, u32[]{:S(2)}) copy-start(bf16[2,256,2048]{2,1,0:T(8,128)(2,1)} %param.18) | copy-start | bytes 6291460
  1929.9 42.1 %copy-start.19 = (f32[2048]{0:T(1024)S(1)}, f32[2048]{0:T(1024)}, u32[]{:S(2)}) copy-start(f32[2048]{0:T(1024)} %copy-done.18) | copy-start | bytes 24580
  1929.9 42.1 %copy-start.22 = (f32[1,2,2,128]{3,1,2,0:T(2,128)S(1)}, f32[1,2,2,128]{3,1,2,0:T(2,128)}, u32[]{:S(2)}) copy-start(f32[1,2,2,128]{3,1,2,0:T(2,128)} %copy-done.21) | copy-start | bytes 6148
  1929.9 42.0 %copy-start.24 = (f32[1,2,2,128]{3,1,2,0:T(2,128)S(1)}, f32[1,2,2,128]{3,1,2,0:T(2,128)}, u32[]{:S(2)}) copy-start(f32[1,2,2,128]{3,1,2,0:T(2,128)} %copy-done.23) | copy-start | bytes 6148
  1930.6 45.0 %copy-start.27 = (f32[4096]{0:T(1024)S(1)}, f32[4096]{0:T(1024)}, u32[]{:S(2)}) copy-start(f32[4096]{0:T(1024)} %get-tuple-element.28) | copy-start | bytes 49156
  1930.6 45.0 %copy-start.28 = (f32[1024]{0:T(1024)S(1)}, f32[1024]{0:T(1024)}, u32[]{:S(2)}) copy-start(f32[1024]{0:T(1024)} %get-tuple-element.30) | copy-start | bytes 12292
  (6 other events, 4.1 us)
Sparse Core Ops, SparseCore 0:
  9.9 55.3 all-gather.8
  67.2 52.6 all-gather.14
  121.8 52.6 all-gather.12
  176.2 52.6 all-gather.18
  230.9 80.7 all-gather.10
  313.7 79.0 all-gather.16
  394.7 155.5 all-gather.20
  552.2 157.4 all-gather.22
  712.0 280.2 reduce-scatter.2
  1100.6 829.2 reduce-scatter.4
  1933.0 38.8 all-reduce.6
  1974.3 836.1 all-reduce.4
where the time goes:
time: 2840 us
  waiting for transfers between devices  2240 us (79%)
  matrix products  263 us (9%)
  other arithmetic  148 us (5%)
  local copies, waits for them, and re-layouts  84.7 us (3%)
  blocking collectives  82.3 us (3%)
    reduce_scatter x1, waiting for transfers between devices, local(): lax.psum_scatter(jnp.concatenate([left_part, right_part], axis=1), 'fsdp'...  774 us
    psum x1, waiting for transfers between devices, local(): weight_grads = lax.psum(scattered, 'ctx')  746 us
    reduce_scatter x1, waiting for transfers between devices, local(): lax.psum_scatter(jnp.concatenate([grad_key_part.reshape(row_count, seq_co...  238 us
    all_gather x1, waiting for transfers between devices, local(): lax.all_gather(down_weight, 'fsdp', axis=0, tiled=True)  140 us
    psum x1, blocking collectives, local(): lax.psum((small_terms[0], small_terms[1], small_terms[2], small_terms[3],...  82.3 us
    all_gather x1, waiting for transfers between devices, local(): lax.all_gather(key_rot, 'ctx', axis=1, tiled=True)  74.9 us
    all_gather x1, waiting for transfers between devices, local(): lax.all_gather(value_rows, 'ctx', axis=1, tiled=True)  69.7 us
    concatenate x1, other arithmetic, local(): jnp.concatenate([left_part, right_part], axis=1)  65.5 us
  transfers between devices with their start and end apart: 12, of which 11 were waited for; matrix products, arithmetic and copies ran while one was open for 13% of the time, Pallas kernels for 0%

commit v1 on v0

--- a/solution.py
+++ b/solution.py
@@ -8,6 +8,15 @@
 SEQ_LEN = 1024
 masked_fill = -1e30
 norm_eps = 1e-05
+
+
+def get_scenes(my_data, row_axis):
+    n_shards = lax.axis_size(row_axis)
+    state_now = my_data
+    for s in [ix for ix in (1, 2, 4, 8, 16) if ix < n_shards]:
+        long_array = lax.ppermute(state_now, row_axis, [(dev, dev ^ s) for dev in range(n_shards)])
+        state_now = state_now + long_array
+    return state_now
 
 
 def positions(group_order, row_start, row_count, group_len):
@@ -268,7 +277,7 @@
     scattered = lax.psum_scatter(
         jnp.concatenate([left_part, right_part], axis=1), "fsdp", scatter_dimension=0, tiled=True
     )
-    weight_grads = lax.psum(scattered, "ctx")
+    weight_grads = get_scenes(scattered, "ctx")
     edge_two = 2 * inner_width
     edge_three = 3 * inner_width
     edge_four = edge_three + hidden_units

time: 2840 us -> 3700 us (1.30)
  blocking collectives: 82.3 us -> 1050 us
  waiting for transfers between devices: 2240 us -> 2090 us
  other arithmetic: 148 us -> 192 us
    psum x1, blocking collectives: 82.3 us -> 1050 us  [local(): lax.psum((small_terms[0], small_terms[1], small_terms[2], small_terms[3],...]
    psum x1 -> x0, waiting for transfers between devices: 746 us -> none  [local(): weight_grads = lax.psum(scattered, 'ctx')]
    ppermute x0 -> x2, waiting for transfers between devices: none -> 540 us  [get_scenes(): lax.ppermute(state_now, row_axis, [(dev, dev ^ s) for dev in range(n_shar...]
    reduce_scatter x1, waiting for transfers between devices: 774 us -> 829 us  [local(): lax.psum_scatter(jnp.concatenate([left_part, right_part], axis=1), 'fsdp'...]
    add x0 -> x2, other arithmetic: none -> 43.5 us  [get_scenes(): state_now = state_now + long_array]
  transfers between devices with their start and end apart: 12 -> 13, of which waited for: 11 -> 11; matrix products, arithmetic and copies ran while one was open for 13% -> 10% of each run, Pallas kernels for 0% -> 0%
where the time goes in v1:
time: 3700 us; the launch traced here: 3690 us
  waiting for transfers between devices  2090 us (56%)
  blocking collectives  1050 us (28%)
  matrix products  262 us (7%)
  other arithmetic  192 us (5%)
  local copies, waits for them, and re-layouts  83.6 us (2%)
    psum x1, blocking collectives, local(): lax.psum((small_terms[0], small_terms[1], small_terms[2], small_terms[3],...  1050 us
    reduce_scatter x1, waiting for transfers between devices, local(): lax.psum_scatter(jnp.concatenate([left_part, right_part], axis=1), 'fsdp'...  829 us
    ppermute x2, waiting for transfers between devices, get_scenes(): lax.ppermute(state_now, row_axis, [(dev, dev ^ s) for dev in range(n_shar...  540 us
    reduce_scatter x1, waiting for transfers between devices, local(): lax.psum_scatter(jnp.concatenate([grad_key_part.reshape(row_count, seq_co...  238 us
    all_gather x1, waiting for transfers between devices, local(): lax.all_gather(down_weight, 'fsdp', axis=0, tiled=True)  140 us
    all_gather x1, waiting for transfers between devices, local(): lax.all_gather(key_rot, 'ctx', axis=1, tiled=True)  74.9 us
  transfers between devices with their start and end apart: 13, of which 11 were waited for; matrix products, arithmetic and copies ran while one was open for 10% of the time, Pallas kernels for 0%

profile of v1, /device:TPU:0, one launch (start us, length us, event | category | flops | bytes accessed | tf_op | source)
XLA Modules:
  0.0 3693.7 jit_solution(15389163368561423933)
XLA Ops:
  14.0 51.3 %all-gather.9.cloned.1.call-done = bf16[2048,1024]{1,0:T(8,128)(2,1)} async-done(((bf16[512,1024]{1,0:T(8,128)(2,1)}), bf16[2048,1024]{1,0:T(8,128)(2,1)}) %all-gather.9.cloned.1.call-update) | async-done | bytes 4194320 | tf_op jit(solution)/shard_map/all_gather | solution.py:95
  65.3 6.1 add_convert_fusion
  72.7 47.2 %all-gather.15.cloned.1.call-done = bf16[2048,1024]{1,0:T(8,128)(2,1)} async-done(((bf16[512,1024]{1,0:T(8,128)(2,1)}), bf16[2048,1024]{1,0:T(8,128)(2,1)}) %all-gather.15.cloned.1.call-update) | async-done | bytes 4194320 | tf_op jit(solution)/shard_map/all_gather | solution.py:94
  119.9 5.8 convolution_add_fusion.1
  128.6 3.7 reshape.388
  134.8 39.8 %all-gather.13.cloned.1.call-done = bf16[2048,1024]{1,0:T(8,128)(2,1)} async-done(((bf16[512,1024]{1,0:T(8,128)(2,1)}), bf16[2048,1024]{1,0:T(8,128)(2,1)}) %all-gather.13.cloned.1.call-update) | async-done | bytes 4194320 | tf_op jit(solution)/shard_map/all_gather | solution.py:93
  174.5 5.8 convolution_add_fusion.2
  180.3 4.5 reshape.399
  184.9 8.3 fusion.57
  193.2 3.6 copy.98
  210.8 18.2 all-gather.19.cloned.1.call-done
  228.9 5.1 convolution_convert_fusion
  242.1 69.6 %all-gather.11.cloned.1.call-done = bf16[2,1024,1024]{2,1,0:T(8,128)(2,1)} async-done(((bf16[2,256,1024]{2,1,0:T(8,128)(2,1)}), bf16[2,1024,1024]{2,1,0:T(8,128)(2,1)}) %all-gather.11.cloned.1.call-update) | async-done | bytes 4194320 | tf_op jit(solution)/shard_map/all_gather | solution.py:135
  311.7 6.2 copy.68
  318.0 74.9 %all-gather.17.cloned.1.call-done = bf16[2,1024,1024]{1,2,0:T(8,128)(2,1)} async-done(((bf16[2,256,1024]{1,2,0:T(8,128)(2,1)}), bf16[2,1024,1024]{1,2,0:T(8,128)(2,1)}) %all-gather.17.cloned.1.call-update) | async-done | bytes 4194320 | tf_op jit(solution)/shard_map/all_gather | solution.py:134
  392.9 20.1 fusion.59
  412.9 14.6 fusion
  427.5 22.3 multiply_reduce_fusion
  449.8 29.6 multiply_convert_fusion
  479.4 12.2 broadcast_multiply_fusion
  491.6 17.0 fusion.2
  508.6 11.9 pad_maximum_fusion.1
  521.1 15.1 fusion.43
  539.8 13.7 multiply_bitcast_fusion
  554.9 14.4 fusion.61
  569.3 140.3 %all-gather.23.cloned.1.call-done = bf16[2048,4096]{1,0:T(8,128)(2,1)} async-done(((bf16[512,4096]{1,0:T(8,128)(2,1)}), bf16[2048,4096]{1,0:T(8,128)(2,1)}) %all-gather.23.cloned.1.call-update) | async-done | bytes 16777232 | tf_op jit(solution)/shard_map/all_gather | solution.py:98
  709.6 22.4 convert_reduce_fusion
  732.1 22.1 convolution_bitcast_fusion
  754.2 238.1 %reduce-scatter.3.cloned.1.call-done = f32[256,2,2048]{0,2,1:T(8,128)} async-done(((f32[1024,2,2048]{0,2,1:T(8,128)}), f32[256,2,2048]{0,2,1:T(8,128)}) %reduce-scatter.3.cloned.1.call-update) | async-done | bytes 4194320 | tf_op jit(solution)/shard_map/reduce_scatter | solution.py:205
  992.3 4.0 convert_reduce_fusion.3
  1008.6 26.3 fusion.13
  1034.9 65.5 %pad_maximum_fusion = f32[2048,12288]{1,0:T(8,128)} fusion(f32[2048,5120]{1,0:T(8,128)} %convolution_bitcast_fusion, f32[2048,7168]{1,0:T(8,128)} %fusion.13), kind=kLoop, calls=%fused_computation | loop fusion | flops 25165824 | bytes 201326592 | tf_op jit(solution)/shard_map/concatenate | solution.py:278
  1100.5 829.4 %reduce-scatter.5.cloned.1.call-done = f32[512,12288]{1,0:T(8,128)} async-done(((f32[2048,12288]{1,0:T(8,128)}), f32[512,12288]{1,0:T(8,128)}) %reduce-scatter.5.cloned.1.call-update) | async-done | bytes 25165840 | tf_op jit(solution)/shard_map/reduce_scatter | solution.py:277
  1931.3 540.5 %collective-permute-done = f32[512,12288]{1,0:T(8,128)S(1)} collective-permute-done((f32[512,12288]{1,0:T(8,128)}, f32[512,12288]{1,0:T(8,128)S(1)}, u32[]{:S(2)}, u32[]{:S(2)}) %collective-permute-start) | collective-permute-done | bytes 25165856 | tf_op jit(solution)/shard_map/ppermute | solution.py:17
  2471.8 17.7 add.232
  2491.9 6.6 fusion.60
  2498.5 15.9 convolution_add_fusion
  2514.4 4.4 fusion.63
  2518.8 4.4 fusion.62
  2523.2 4.4 fusion.64
  2527.6 17.7 add_add_fusion
  2548.1 34.4 all-reduce.4.cloned.1.call-done
  2582.6 3.9 fusion.38
  2586.5 1049.2 %all-reduce = (f32[2048]{0:T(1024)}, f32[2048]{0:T(1024)}, f32[1024]{0:T(1024)}, f32[1024]{0:T(1024)}, f32[1024]{0:T(1024)}, /*index=5*/f32[4096]{0:T(1024)}, f32[2048]{0:T(1024)}) all-reduce(f32[2048]{0:T(1024)S(1)} %get-tuple-element.15, f32[2048]{0:T(1024)S(1)} %get-tuple-element.18, ...), channel_id=1, replica_groups=mesh['fsdp'=4,'ctx'=4,'tp'=2] {'fsdp','ctx'}, use_global_device_ids=true, to_apply=%region_13.14 | all-reduce | flops 13312 | bytes 106496 | tf_op jit(solution)/shard_map/psum | solution.py:261
  3635.6 6.8 fusion.37
  3642.4 25.8 add.233
  3668.2 7.5 fusion.56
  3675.7 11.1 fusion.55
  (169 shorter events, 59.5 us)
Async XLA Ops:
  7.2 2.9 copy-start
  7.2 4.0 copy-start.34
  7.2 4.0 copy-start.30
  7.2 4.0 copy-start.31
  7.2 58.1 %all-gather.9.cloned.1.call-start = ((), (), s32[]{:S(2)}) async-start(), calls=%async_computation.2 | async-start | bytes 5242880 | tf_op jit(solution)/shard_map/all_gather | solution.py:95
  8.0 112.0 %all-gather.15.cloned.1.call-start = ((), (), s32[]{:S(2)}) async-start(), calls=%async_computation.5 | async-start | bytes 5242880 | tf_op jit(solution)/shard_map/all_gather | solution.py:94
  8.7 165.8 %all-gather.13.cloned.1.call-start = ((), (), s32[]{:S(2)}) async-start(), calls=%async_computation.4 | async-start | bytes 5242880 | tf_op jit(solution)/shard_map/all_gather | solution.py:93
  9.4 219.5 %all-gather.19.cloned.1.call-start = ((), (), s32[]{:S(2)}) async-start(), calls=%async_computation.7 | async-start | bytes 5242880 | tf_op jit(solution)/shard_map/all_gather | solution.py:96
  10.0 301.7 %all-gather.11.cloned.1.call-start = ((), (), s32[]{:S(2)}) async-start(), calls=%async_computation.3 | async-start | bytes 5242880 | tf_op jit(solution)/shard_map/all_gather | solution.py:135
  14.0 57.8 %copy-start.35 = (bf16[1024]{0:T(1024)(128)(2,1)S(1)}, bf16[1024]{0:T(1024)(128)(2,1)}, u32[]{:S(2)}) copy-start(bf16[1024]{0:T(1024)(128)(2,1)} %param.25) | copy-start | bytes 6148
  14.0 57.8 %copy-start.36 = (bf16[1024]{0:T(1024)(128)(2,1)S(1)}, bf16[1024]{0:T(1024)(128)(2,1)}, u32[]{:S(2)}) copy-start(bf16[1024]{0:T(1024)(128)(2,1)} %param.27) | copy-start | bytes 6148
  14.0 57.9 %copy-start.37 = (s32[8]{0:T(128)S(1)}, s32[8]{0:T(128)}, u32[]{:S(2)}) copy-start(s32[8]{0:T(128)} %param.21) | copy-start | bytes 100
  14.0 105.9 %copy-start.3 = (bf16[512,2048]{1,0:T(8,128)(2,1)S(1)}, bf16[512,2048]{1,0:T(8,128)(2,1)}, u32[]{:S(2)}) copy-start(bf16[512,2048]{1,0:T(8,128)(2,1)} %fusion.32) | copy-start | bytes 6291460
  71.5 321.4 %all-gather.17.cloned.1.call-start = ((), (), s32[]{:S(2)}) async-start(), calls=%async_computation.6 | async-start | bytes 5242880 | tf_op jit(solution)/shard_map/all_gather | solution.py:134
  72.7 128.0 %copy-start.16 = (f32[256,16]{0,1:T(8,128)}, f32[256,16]{0,1:T(8,128)S(1)}, u32[]{:S(2)}) copy-start(f32[256,16]{0,1:T(8,128)S(1)} %get-tuple-element.68) | copy-start | bytes 49156
  193.2 7.1 copy-start.5
  200.3 2.0 copy-start.15
  204.9 1.7 copy-start.38
  205.0 349.9 %all-gather.21.cloned.1.call-start = ((), (), s32[]{:S(2)}) async-start(), calls=%async_computation.8 | async-start | bytes 20971520 | tf_op jit(solution)/shard_map/all_gather | solution.py:97
  205.7 503.9 %all-gather.23.cloned.1.call-start = ((), (), s32[]{:S(2)}) async-start(), calls=%async_computation.9 | async-start | bytes 20971520 | tf_op jit(solution)/shard_map/all_gather | solution.py:98
  206.5 785.9 %reduce-scatter.3.cloned.1.call-start = ((), (), s32[]{:S(2)}) async-start(), calls=%async_computation.10 | async-start | bytes 20971520 | tf_op jit(solution)/shard_map/reduce_scatter | solution.py:205
  242.1 150.7 %copy-start.7 = (bf16[2,256,16,32]{1,3,2,0:T(8,128)(2,1)S(1)}, bf16[2,256,16,32]{1,3,2,0:T(8,128)(2,1)}, u32[]{:S(2)}) copy-start(bf16[2,256,16,32]{1,3,2,0:T(8,128)(2,1)} %copy.99) | copy-start | bytes 1572868
  242.1 150.7 %copy-start.8 = (pred[2,256,1024]{2,1,0:T(8,128)(4,1)S(1)}, pred[2,256,1024]{2,1,0:T(8,128)(4,1)}, u32[]{:S(2)}) copy-start(pred[2,256,1024]{2,1,0:T(8,128)(4,1)} %broadcast_or_fusion) | copy-start | bytes 1572868
  242.1 150.7 %copy-start.14 = (bf16[2,256,16,16]{1,3,2,0:T(8,128)(2,1)S(1)}, bf16[2,256,16,16]{1,3,2,0:T(8,128)(2,1)}, u32[]{:S(2)}) copy-start(bf16[2,256,16,16]{1,3,2,0:T(8,128)(2,1)} %get-tuple-element.57) | copy-start | bytes 786436
  412.9 14.6 copy-start.2
  520.4 1409.4 %reduce-scatter.5.cloned.1.call-start = ((), (), s32[]{:S(2)}) async-start(), calls=%async_computation.11 | async-start | bytes 125829120 | tf_op jit(solution)/shard_map/reduce_scatter | solution.py:277
  539.8 15.0 copy-start.4
  754.2 242.3 %copy-start.17 = (f32[256,16]{0,1:T(8,128)S(1)}, f32[256,16]{0,1:T(8,128)}, u32[]{:S(2)}) copy-start(f32[256,16]{0,1:T(8,128)} %copy-done.16) | copy-start | bytes 49156
  754.2 242.3 %copy-start.20 = (f32[256,16]{0,1:T(8,128)S(1)}, f32[256,16]{0,1:T(8,128)}, u32[]{:S(2)}) copy-start(f32[256,16]{0,1:T(8,128)} %get-tuple-element.66) | copy-start | bytes 49156
  992.3 4.1 copy-start.6
  1000.0 7.1 copy-start.11
  1100.4 1391.5 %copy-start.10 = (bf16[128,8,2,256]{3,1,2,0:T(8,128)(2,1)S(1)}, bf16[128,8,2,256]{3,1,2,0:T(8,128)(2,1)}, u32[]{:S(2)}) copy-start(bf16[128,8,2,256]{3,1,2,0:T(8,128)(2,1)} %copy-done.9) | copy-start | bytes 3145732
  1100.4 1482.1 %all-reduce.4.cloned.1.call-start = ((), (), s32[]{:S(2)}) async-start(), calls=%async_computation.12 | async-start | bytes 16777216 | tf_op jit(solution)/shard_map/psum | solution.py:162
  1929.8 541.9 %collective-permute-start = (f32[512,12288]{1,0:T(8,128)}, f32[512,12288]{1,0:T(8,128)S(1)}, u32[]{:S(2)}, u32[]{:S(2)}) collective-permute-start(f32[512,12288]{1,0:T(8,128)} %reduce-scatter.5.cloned.1.call-done), channel_id=1, source_target_pairs={{0,2},{2,0},{4,6},{6,4},{1,3},{3,1},{5,7},{7,5},{8,10},{10,8},{12,... | collective-permute-start | bytes 75497480 | tf_op jit(solution)/shard_map/ppermute | solution.py:17
  2489.5 1152.9 %collective-permute-start.1 = (f32[512,12288]{1,0:T(8,128)}, f32[512,12288]{1,0:T(8,128)}, u32[]{:S(2)}, u32[]{:S(2)}) collective-permute-start(f32[512,12288]{1,0:T(8,128)} %add.232), channel_id=1, source_target_pairs={{0,4},{2,6},{4,0},{6,2},{1,5},{3,7},{5,1},{7,3},{8,12},{10,14},{12... | collective-permute-start | bytes 75497480 | tf_op jit(solution)/shard_map/ppermute | solution.py:17
  2498.5 15.9 copy-start.12
  2498.5 15.9 copy-start.40
  2514.4 4.4 copy-start.13
  2514.4 4.4 copy-start.41
  2518.8 4.4 copy-start.39
  2545.3 2.7 copy-start.26
  2545.3 2.8 copy-start.25
  2545.3 37.3 %copy-start.1 = (bf16[2,256,2048]{2,1,0:T(8,128)(2,1)S(1)}, bf16[2,256,2048]{2,1,0:T(8,128)(2,1)}, u32[]{:S(2)}) copy-start(bf16[2,256,2048]{2,1,0:T(8,128)(2,1)} %param.18) | copy-start | bytes 6291460
  2545.3 37.3 %copy-start.19 = (f32[2048]{0:T(1024)S(1)}, f32[2048]{0:T(1024)}, u32[]{:S(2)}) copy-start(f32[2048]{0:T(1024)} %copy-done.18) | copy-start | bytes 24580
  2545.3 37.2 %copy-start.22 = (f32[1,2,2,128]{3,1,2,0:T(2,128)S(1)}, f32[1,2,2,128]{3,1,2,0:T(2,128)}, u32[]{:S(2)}) copy-start(f32[1,2,2,128]{3,1,2,0:T(2,128)} %copy-done.21) | copy-start | bytes 6148
  2545.3 37.2 %copy-start.24 = (f32[1,2,2,128]{3,1,2,0:T(2,128)S(1)}, f32[1,2,2,128]{3,1,2,0:T(2,128)}, u32[]{:S(2)}) copy-start(f32[1,2,2,128]{3,1,2,0:T(2,128)} %copy-done.23) | copy-start | bytes 6148
  2546.0 40.5 %copy-start.27 = (f32[4096]{0:T(1024)S(1)}, f32[4096]{0:T(1024)}, u32[]{:S(2)}) copy-start(f32[4096]{0:T(1024)} %get-tuple-element.28) | copy-start | bytes 49156
  2546.0 40.5 %copy-start.28 = (f32[1024]{0:T(1024)S(1)}, f32[1024]{0:T(1024)}, u32[]{:S(2)}) copy-start(f32[1024]{0:T(1024)} %get-tuple-element.30) | copy-start | bytes 12292
  (7 other events, 5.0 us)
Sparse Core Ops, SparseCore 0:
  9.9 55.3 all-gather.8
  67.2 52.6 all-gather.14
  121.8 52.6 all-gather.12
  176.2 52.6 all-gather.18
  230.9 80.7 all-gather.10
  313.7 79.0 all-gather.16
  394.7 155.5 all-gather.20
  552.2 157.4 all-gather.22
  712.0 280.2 reduce-scatter.2
  1100.5 829.2 reduce-scatter.4
  2545.5 37.0 all-reduce.3
